TPU v7x, 32 devices: a whole 2x2x4 slice. The times are simulated.
32 devices in a mesh: groups: 2 (over y), blk: 4 (over z), head: 2 (over x), rep: 2 (over core).
Axes of the slice: x: 2, y: 2, z: 4, core: 2. Of those that a mesh axis runs over, the one named last changes fastest.
Arguments:
- query: bfloat16 [128, 16384], P(('groups', 'blk', 'rep'), 'head'), parts along dimension 0, may hold values from -200 to 200
- keys: bfloat16 [8, 2, 2048, 8, 128], P(('groups', 'blk'), 'rep', None, 'head'), parts along dimension 0, may hold values from -8 to 8
- values: bfloat16 [8, 2, 2048, 8, 128], P(('groups', 'blk'), 'rep', None, 'head'), parts along dimension 0, may hold values from -6 to 6
- lengths: int32 [128], P('groups'), parts along dimension 0, may hold values from 2 to 8192, as said below
- out_weight: bfloat16 [16384, 16384], P('head', ('blk', 'rep')), may hold values from -0.046875 to 0.046875
Outputs:
- projected: bfloat16 [128, 16384], P(('groups', 'head'), ('blk', 'rep')), parts along dimension 0
There are 2 independent parts, one for each index of `groups`. A program takes and returns all parts, laid end to end along the dimension named above; an argument that names none is the same for every part. Nothing has to cross between parts.
Inputs may be any that keep to these rules, and one draw needn't show every extreme that they name: `lengths`: some request of every draw sees all 8192 positions.
All inputs are finite; a program needn't handle non-finite values.
Results may differ from a plain program's by a relative error of at most 0.012.
Values may be sent and summed in bfloat16 or wider, within the bound.
A program may use at most 128 MiB of HBM per device.

v0:
```python
import jax
import jax.numpy as jnp
from jax import lax
from jax.sharding import PartitionSpec as P

NEG = -1e30


def shifted(x, axis, by):
    devices = lax.axis_size(axis)
    return lax.ppermute(x, axis, [(i, (i + by) % devices) for i in range(devices)])


def stop_partial(visiting, row_lengths, positions, key_slot, value_slot, score_scale):
    row_count = visiting.shape[0]
    kv_heads = key_slot.shape[1]
    head_dim = key_slot.shape[2]
    queries = visiting.reshape(row_count, kv_heads, -1, head_dim)
    scores = (
        jnp.einsum("rkgd,jkd->rkgj", queries, key_slot, preferred_element_type=jnp.float32)
        * score_scale
    )
    live_mask = (positions[None, :] < row_lengths[:, None])[:, None, None, :]
    best_score = jnp.max(jnp.where(live_mask, scores, NEG), axis=-1)
    weights = jnp.where(live_mask, jnp.exp(scores - best_score[..., None]), 0.0)
    block_sum = jnp.sum(weights, axis=-1)
    partial_value = jnp.einsum(
        "rkgj,jkd->rkgd",
        weights.astype(jnp.bfloat16),
        value_slot,
        preferred_element_type=jnp.float32,
    )
    return (partial_value.astype(jnp.bfloat16), best_score, block_sum)


def body(query, keys, values, lengths, out_weight):
    row_count = query.shape[0]
    slab_len = keys.shape[2]
    head_dim = keys.shape[4]
    score_scale = head_dim ** (-0.5)
    blocks = lax.axis_size("blk")
    replicas = lax.axis_size("rep")
    span_count = min(8, blocks)
    stride = blocks // span_count
    holder = lax.axis_index("blk")
    rep_index = lax.axis_index("rep")
    key_slot = keys[0, 0]
    value_slot = values[0, 0]
    positions = holder // stride * slab_len + jnp.arange(slab_len, dtype=jnp.int32)
    visiting = query
    stored = []
    for stop_index in range(span_count):
        if stop_index > 0:
            visiting = shifted(visiting, "blk", stride)
        owner_index = (holder - stop_index * stride) % blocks
        first_row = (owner_index * replicas + rep_index) * row_count
        row_lengths = lax.dynamic_slice_in_dim(lengths, first_row, row_count, 0)
        stop_piece = stop_partial(
            visiting, row_lengths, positions, key_slot, value_slot, score_scale
        )
        stored.append(stop_piece)
    outs_home = [stored[0][0]]
    best_home = [stored[0][1]]
    sums_home = [stored[0][2]]
    for stop_index in range(1, span_count):
        outs_home.append(shifted(stored[stop_index][0], "blk", -stop_index * stride))
        stats_home = shifted(
            (stored[stop_index][1], stored[stop_index][2]), "blk", -stop_index * stride
        )
        best_home.append(stats_home[0])
        sums_home.append(stats_home[1])
    best_all = jnp.stack(best_home)
    overall = jnp.max(best_all, axis=0)
    factors = jnp.exp(best_all - overall[None])
    total_sum = jnp.sum(factors * jnp.stack(sums_home), axis=0)
    total_out = jnp.sum(factors[..., None] * jnp.stack(outs_home).astype(jnp.float32), axis=0)
    attended = (total_out / total_sum[..., None]).astype(jnp.bfloat16).reshape(row_count, -1)
    gathered = lax.all_gather(attended, ("blk", "rep"), axis=0, tiled=True)
    projected = lax.psum_scatter(
        jnp.dot(gathered, out_weight, preferred_element_type=jnp.float32),
        "head",
        scatter_dimension=0,
        tiled=True,
    )
    return projected.astype(jnp.bfloat16)


def solution(mesh):
    return jax.shard_map(
        body,
        mesh=mesh,
        in_specs=(
            P(("groups", "blk", "rep"), "head"),
            P(("groups", "blk"), "rep", None, "head", None),
            P(("groups", "blk"), "rep", None, "head", None),
            P("groups"),
            P("head", ("blk", "rep")),
        ),
        out_specs=P(("groups", "head"), ("blk", "rep")),
        check_vma=False,
    )
```

profile of v0, /device:TPU:0, one launch (start us, length us, event | category | flops | bytes accessed | tf_op | source)
XLA Modules:
  0.0 113.8 jit_solution(224056178729096985)
XLA Ops:
  6.5 0.0 copy-start
  6.5 0.0 all-gather.2.cloned.1.call-start
  6.5 3.1 %collective-permute-start = (bf16[8,8192]{1,0:T(8,128)(2,1)}, bf16[8,8192]{1,0:T(8,128)(2,1)S(1)}, u32[]{:S(2)}, u32[]{:S(2)}) collective-permute-start(bf16[8,8192]{1,0:T(8,128)(2,1)} %param.5), channel_id=1, source_target_pairs={{0,4},{4,8},{8,12},{12,0},{1,5},{5,9},{9,13},{13,1},{2,6},{6,10},{... | collective-permute-start | bytes 393224 | tf_op jit(solution)/shard_map/ppermute | solution.py:11
  9.6 0.9 fusion.111
  10.5 0.1 broadcast_compare_fusion.3
  10.6 2.7 %fusion.9 = (f32[8,4,16]{2,0,1:T(8,128)S(1)}, f32[4,2048,8,16]{1,3,2,0:T(8,128)S(1)}) fusion(pred[8,2048]{1,0:T(8,128)(4,1)S(1)} %get-tuple-element.7, bf16[8,4,16,128]{3,0,2,1:T(8,128)(2,1)} %bitcast.149, bf16[2048,4,128,1]{2,1,0,3:T(4,128)(2,1)} %bitcast.145), kind=kOutput, calls=%fused_computation.17 | convolution fusion | flops 271580672 | bytes 6440960 | tf_op jit(solution)/shard_map/rkgd,jkd->rkgj/dot_general | solution.py:20
  13.3 0.0 copy-done
  13.3 1.2 %fusion.91 = bf16[1,8,4,16,128]{4,3,1,2,0:T(8,128)(2,1)S(1)} fusion(bf16[2048,4,128,1]{2,1,0,3:T(4,128)(2,1)S(1)} %bitcast.122, f32[4,2048,8,16]{1,3,2,0:T(8,128)S(1)} %get-tuple-element.22, f32[8,4,16]{2,0,1:T(8,128)S(1)} %get-tuple-element.21, pred[8,2048]{1,0:T(8,128)(4,1)S(1)} %get-tuple-element.7), kind=kOutput, calls=%fused_computation.67 | convolution fusion | flops 272695296 | bytes 6440960 | tf_op jit(solution)/shard_map/rkgj,jkd->rkgd/dot_general | solution.py:27
  14.5 0.0 copy-start.1
  14.6 1.1 fusion.12
  15.7 0.0 collective-permute-done
  15.7 0.4 copy-done.1
  16.1 1.1 fusion.6
  17.3 1.2 %fusion.86 = bf16[8,4,16,128]{3,2,0,1:T(8,128)(2,1)S(1)} fusion(bf16[2048,4,128,1]{2,1,0,3:T(4,128)(2,1)S(1)} %bitcast.125, f32[4,2048,8,16]{1,3,2,0:T(8,128)S(1)} %get-tuple-element.20, f32[8,4,16]{2,0,1:T(8,128)S(1)} %get-tuple-element.19, pred[8,2048]{1,0:T(8,128)(4,1)S(1)} %get-tuple-element.8), kind=kOutput, calls=%fused_computation.66 | convolution fusion | flops 272695296 | bytes 6440960 | tf_op jit(solution)/shard_map/rkgj,jkd->rkgd/dot_general | solution.py:27
  18.5 1.6 %collective-permute-start.2 = (bf16[8,8192]{1,0:T(8,128)(2,1)S(1)}, bf16[8,8192]{1,0:T(8,128)(2,1)S(1)}, u32[]{:S(2)}, u32[]{:S(2)}) collective-permute-start(bf16[8,8192]{1,0:T(8,128)(2,1)S(1)} %collective-permute-done), channel_id=1, source_target_pairs={{0,4},{4,8},{8,12},{12,0},{1,5},{5,9},{9,13},{13,1},{2,6},{6,10},{... | collective-permute-start | bytes 393224 | tf_op jit(solution)/shard_map/ppermute | solution.py:11
  20.1 1.1 fusion.14
  21.2 2.3 %collective-permute-start.1 = (f32[8,4,16]{2,0,1:T(8,128)S(1)}, f32[8,4,16]{2,0,1:T(8,128)S(1)}, u32[]{:S(2)}, u32[]{:S(2)}) collective-permute-start(f32[8,4,16]{2,0,1:T(8,128)S(1)} %get-tuple-element.19), channel_id=1, source_target_pairs={{0,12},{4,0},{8,4},{12,8},{1,13},{5,1},{9,5},{13,9},{2,14},{6,2},{... | collective-permute-start | bytes 6152 | tf_op jit(solution)/shard_map/ppermute | solution.py:11
  23.5 0.3 collective-permute-start.9
  23.8 2.0 %collective-permute-start.6 = (bf16[8,4,16,128]{3,2,0,1:T(8,128)(2,1)S(1)}, bf16[8,4,16,128]{3,2,0,1:T(8,128)(2,1)S(1)}, u32[]{:S(2)}, u32[]{:S(2)}) collective-permute-start(bf16[8,4,16,128]{3,2,0,1:T(8,128)(2,1)S(1)} %fusion.86), channel_id=1, source_target_pairs={{0,12},{4,0},{8,4},{12,8},{1,13},{5,1},{9,5},{13,9},{2,14},{6,2},{... | collective-permute-start | bytes 393224 | tf_op jit(solution)/shard_map/ppermute | solution.py:11
  25.8 0.0 collective-permute-done.2
  25.8 1.1 fusion.3
  26.9 1.2 %fusion.81 = bf16[8,4,16,128]{3,2,0,1:T(8,128)(2,1)S(1)} fusion(bf16[2048,4,128,1]{2,1,0,3:T(4,128)(2,1)S(1)} %bitcast.124, f32[4,2048,8,16]{1,3,2,0:T(8,128)S(1)} %get-tuple-element.18, f32[8,4,16]{2,0,1:T(8,128)S(1)} %get-tuple-element.17, pred[8,2048]{1,0:T(8,128)(4,1)S(1)} %get-tuple-element.9), kind=kOutput, calls=%fused_computation.65 | convolution fusion | flops 272695296 | bytes 6440960 | tf_op jit(solution)/shard_map/rkgj,jkd->rkgd/dot_general | solution.py:27
  28.2 0.3 collective-permute-start.4
  28.4 1.1 fusion.16
  29.5 1.2 %collective-permute-start.3 = (f32[8,4,16]{2,0,1:T(8,128)S(1)}, f32[8,4,16]{2,0,1:T(8,128)S(1)}, u32[]{:S(2)}, u32[]{:S(2)}) collective-permute-start(f32[8,4,16]{2,0,1:T(8,128)S(1)} %get-tuple-element.17), channel_id=1, source_target_pairs={{0,8},{4,12},{8,0},{12,4},{1,9},{5,13},{9,1},{13,5},{2,10},{6,14},... | collective-permute-start | bytes 6152 | tf_op jit(solution)/shard_map/ppermute | solution.py:11
  30.8 4.5 %collective-permute-done.4 = bf16[8,8192]{1,0:T(8,128)(2,1)S(1)} collective-permute-done((bf16[8,8192]{1,0:T(8,128)(2,1)S(1)}, bf16[8,8192]{1,0:T(8,128)(2,1)S(1)}, u32[]{:S(2)}, u32[]{:S(2)}) %collective-permute-start.4) | collective-permute-done | bytes 131104 | tf_op jit(solution)/shard_map/ppermute | solution.py:11
  35.3 1.1 fusion
  36.4 0.1 collective-permute-start.5
  36.5 1.2 %fusion.76 = bf16[8,4,16,128]{3,2,0,1:T(8,128)(2,1)S(1)} fusion(bf16[2048,4,128,1]{2,1,0,3:T(4,128)(2,1)S(1)} %bitcast.123, f32[4,2048,8,16]{1,3,2,0:T(8,128)S(1)} %get-tuple-element.16, f32[8,4,16]{2,0,1:T(8,128)S(1)} %get-tuple-element.15, pred[8,2048]{1,0:T(8,128)(4,1)S(1)} %get-tuple-element.10), kind=kOutput, calls=%fused_computation.64 | convolution fusion | flops 272695296 | bytes 6440960 | tf_op jit(solution)/shard_map/rkgj,jkd->rkgd/dot_general | solution.py:27
  37.7 1.1 fusion.18
  38.8 0.0 collective-permute-done.1
  38.8 0.2 collective-permute-start.10
  39.0 0.0 collective-permute-done.3
  39.0 2.8 %collective-permute-start.7 = (bf16[8,4,16,128]{3,2,0,1:T(8,128)(2,1)S(1)}, bf16[8,4,16,128]{3,2,0,1:T(8,128)(2,1)S(1)}, u32[]{:S(2)}, u32[]{:S(2)}) collective-permute-start(bf16[8,4,16,128]{3,2,0,1:T(8,128)(2,1)S(1)} %fusion.81), channel_id=1, source_target_pairs={{0,8},{4,12},{8,0},{12,4},{1,9},{5,13},{9,1},{13,5},{2,10},{6,14},... | collective-permute-start | bytes 393224 | tf_op jit(solution)/shard_map/ppermute | solution.py:11
  41.8 0.3 collective-permute-done.5
  42.1 1.2 %collective-permute-start.11 = (f32[8,4,16]{2,0,1:T(8,128)S(1)}, f32[8,4,16]{2,0,1:T(8,128)S(1)}, u32[]{:S(2)}, u32[]{:S(2)}) collective-permute-start(f32[8,4,16]{2,0,1:T(8,128)S(1)} %fusion.18), channel_id=1, source_target_pairs={{0,4},{4,8},{8,12},{12,0},{1,5},{5,9},{9,13},{13,1},{2,6},{6,10},{... | collective-permute-start | bytes 6152 | tf_op jit(solution)/shard_map/ppermute | solution.py:11
  43.3 0.0 collective-permute-done.9
  43.3 0.1 collective-permute-start.8
  43.4 2.8 %collective-permute-done.10 = f32[8,4,16]{2,0,1:T(8,128)S(1)} collective-permute-done((f32[8,4,16]{2,0,1:T(8,128)S(1)}, f32[8,4,16]{2,0,1:T(8,128)S(1)}, u32[]{:S(2)}, u32[]{:S(2)}) %collective-permute-start.10) | collective-permute-done | bytes 2080 | tf_op jit(solution)/shard_map/ppermute | solution.py:11
  46.2 2.6 %collective-permute-done.11 = f32[8,4,16]{2,0,1:T(8,128)S(1)} collective-permute-done((f32[8,4,16]{2,0,1:T(8,128)S(1)}, f32[8,4,16]{2,0,1:T(8,128)S(1)}, u32[]{:S(2)}, u32[]{:S(2)}) %collective-permute-start.11) | collective-permute-done | bytes 2080 | tf_op jit(solution)/shard_map/ppermute | solution.py:11
  48.8 0.0 collective-permute-done.6
  48.9 1.7 %collective-permute-done.7 = bf16[8,4,16,128]{3,2,0,1:T(8,128)(2,1)S(1)} collective-permute-done((bf16[8,4,16,128]{3,2,0,1:T(8,128)(2,1)S(1)}, bf16[8,4,16,128]{3,2,0,1:T(8,128)(2,1)S(1)}, u32[]{:S(2)}, u32[]{:S(2)}) %collective-permute-start.7) | collective-permute-done | bytes 131104 | tf_op jit(solution)/shard_map/ppermute | solution.py:11
  50.6 0.0 collective-permute-done.8
  50.6 0.3 multiply_reduce_fusion
  50.9 0.1 divide_convert_fusion
  51.1 0.7 copy.137
  51.9 0.0 all-gather.2.cloned.1.call-update
  51.9 0.0 reduce-scatter.2.cloned.1.call-start
  51.9 21.4 %all-gather.2.cloned.1.call-done = bf16[64,8192]{1,0:T(8,128)(2,1)} async-done(((bf16[8,8192]{1,0:T(8,128)(2,1)}), bf16[64,8192]{1,0:T(8,128)(2,1)}) %all-gather.2.cloned.1.call-update) | async-done | bytes 1048592 | tf_op jit(solution)/shard_map/all_gather | solution.py:78
  73.3 17.6 %fusion.112 = f32[64,2048]{1,0:T(8,128)} fusion(bf16[64,8192]{1,0:T(8,128)(2,1)} %all-gather.2.cloned.1.call-done, bf16[8192,2048]{1,0:T(8,128)(2,1)} %param.9), kind=kOutput, calls=%fused_computation.94 | convolution fusion | flops 2147483648 | bytes 35127296 | tf_op jit(solution)/shard_map/dot_general | solution.py:80
  91.0 0.0 reduce-scatter.2.cloned.1.call-update
  91.0 14.4 %reduce-scatter.2.cloned.1.call-done = f32[32,2048]{1,0:T(8,128)} async-done(((f32[64,2048]{1,0:T(8,128)}), f32[32,2048]{1,0:T(8,128)}) %reduce-scatter.2.cloned.1.call-update) | async-done | bytes 262160 | tf_op jit(solution)/shard_map/reduce_scatter | solution.py:79
  105.4 1.6 %convert_element_type.64 = bf16[32,2048]{1,0:T(8,128)(2,1)} convert(f32[32,2048]{1,0:T(8,128)} %reduce-scatter.2.cloned.1.call-done) | non-fusion elementwise | flops 65536 | bytes 393216 | tf_op jit(solution)/shard_map/convert_element_type | solution.py:85
  (7 shorter events, 0.1 us)
Async XLA Ops:
  6.5 6.8 %copy-start = (bf16[1,1,2048,4,128]{4,3,2,1,0:T(4,128)(2,1)S(1)}, bf16[1,1,2048,4,128]{4,3,2,1,0:T(4,128)(2,1)}, u32[]{:S(2)}) copy-start(bf16[1,1,2048,4,128]{4,3,2,1,0:T(4,128)(2,1)} %param.7) | copy-start | bytes 6291460
  6.5 66.8 %all-gather.2.cloned.1.call-start = ((), (), s32[]{:S(2)}) async-start(), calls=%async_computation.1 | async-start | bytes 1179648 | tf_op jit(solution)/shard_map/all_gather | solution.py:78
  6.5 9.1 %collective-permute-start = (bf16[8,8192]{1,0:T(8,128)(2,1)}, bf16[8,8192]{1,0:T(8,128)(2,1)S(1)}, u32[]{:S(2)}, u32[]{:S(2)}) collective-permute-start(bf16[8,8192]{1,0:T(8,128)(2,1)} %param.5), channel_id=1, source_target_pairs={{0,4},{4,8},{8,12},{12,0},{1,5},{5,9},{9,13},{13,1},{2,6},{6,10},{... | collective-permute-start | bytes 393224 | tf_op jit(solution)/shard_map/ppermute | solution.py:11
  14.5 1.6 %copy-start.1 = (bf16[1,1,2048,4,128]{4,3,2,1,0:T(4,128)(2,1)S(1)}, bf16[1,1,2048,4,128]{4,3,2,1,0:T(4,128)(2,1)}, u32[]{:S(2)}) copy-start(bf16[1,1,2048,4,128]{4,3,2,1,0:T(4,128)(2,1)} %param.6) | copy-start | bytes 6291460
  18.5 7.3 %collective-permute-start.2 = (bf16[8,8192]{1,0:T(8,128)(2,1)S(1)}, bf16[8,8192]{1,0:T(8,128)(2,1)S(1)}, u32[]{:S(2)}, u32[]{:S(2)}) collective-permute-start(bf16[8,8192]{1,0:T(8,128)(2,1)S(1)} %collective-permute-done), channel_id=1, source_target_pairs={{0,4},{4,8},{8,12},{12,0},{1,5},{5,9},{9,13},{13,1},{2,6},{6,10},{... | collective-permute-start | bytes 393224 | tf_op jit(solution)/shard_map/ppermute | solution.py:11
  21.2 17.6 %collective-permute-start.1 = (f32[8,4,16]{2,0,1:T(8,128)S(1)}, f32[8,4,16]{2,0,1:T(8,128)S(1)}, u32[]{:S(2)}, u32[]{:S(2)}) collective-permute-start(f32[8,4,16]{2,0,1:T(8,128)S(1)} %get-tuple-element.19), channel_id=1, source_target_pairs={{0,12},{4,0},{8,4},{12,8},{1,13},{5,1},{9,5},{13,9},{2,14},{6,2},{... | collective-permute-start | bytes 6152 | tf_op jit(solution)/shard_map/ppermute | solution.py:11
  23.5 19.8 %collective-permute-start.9 = (f32[8,4,16]{2,0,1:T(8,128)S(1)}, f32[8,4,16]{2,0,1:T(8,128)S(1)}, u32[]{:S(2)}, u32[]{:S(2)}) collective-permute-start(f32[8,4,16]{2,0,1:T(8,128)S(1)} %fusion.14), channel_id=1, source_target_pairs={{0,12},{4,0},{8,4},{12,8},{1,13},{5,1},{9,5},{13,9},{2,14},{6,2},{... | collective-permute-start | bytes 6152 | tf_op jit(solution)/shard_map/ppermute | solution.py:11
  23.8 25.0 %collective-permute-start.6 = (bf16[8,4,16,128]{3,2,0,1:T(8,128)(2,1)S(1)}, bf16[8,4,16,128]{3,2,0,1:T(8,128)(2,1)S(1)}, u32[]{:S(2)}, u32[]{:S(2)}) collective-permute-start(bf16[8,4,16,128]{3,2,0,1:T(8,128)(2,1)S(1)} %fusion.86), channel_id=1, source_target_pairs={{0,12},{4,0},{8,4},{12,8},{1,13},{5,1},{9,5},{13,9},{2,14},{6,2},{... | collective-permute-start | bytes 393224 | tf_op jit(solution)/shard_map/ppermute | solution.py:11
  28.2 7.1 %collective-permute-start.4 = (bf16[8,8192]{1,0:T(8,128)(2,1)S(1)}, bf16[8,8192]{1,0:T(8,128)(2,1)S(1)}, u32[]{:S(2)}, u32[]{:S(2)}) collective-permute-start(bf16[8,8192]{1,0:T(8,128)(2,1)S(1)} %collective-permute-done.2), channel_id=1, source_target_pairs={{0,4},{4,8},{8,12},{12,0},{1,5},{5,9},{9,13},{13,1},{2,6},{6,10},{... | collective-permute-start | bytes 393224 | tf_op jit(solution)/shard_map/ppermute | solution.py:11
  29.5 9.4 %collective-permute-start.3 = (f32[8,4,16]{2,0,1:T(8,128)S(1)}, f32[8,4,16]{2,0,1:T(8,128)S(1)}, u32[]{:S(2)}, u32[]{:S(2)}) collective-permute-start(f32[8,4,16]{2,0,1:T(8,128)S(1)} %get-tuple-element.17), channel_id=1, source_target_pairs={{0,8},{4,12},{8,0},{12,4},{1,9},{5,13},{9,1},{13,5},{2,10},{6,14},... | collective-permute-start | bytes 6152 | tf_op jit(solution)/shard_map/ppermute | solution.py:11
  36.4 5.7 %collective-permute-start.5 = (f32[8,4,16]{2,0,1:T(8,128)S(1)}, f32[8,4,16]{2,0,1:T(8,128)S(1)}, u32[]{:S(2)}, u32[]{:S(2)}) collective-permute-start(f32[8,4,16]{2,0,1:T(8,128)S(1)} %get-tuple-element.15), channel_id=1, source_target_pairs={{0,4},{4,8},{8,12},{12,0},{1,5},{5,9},{9,13},{13,1},{2,6},{6,10},{... | collective-permute-start | bytes 6152 | tf_op jit(solution)/shard_map/ppermute | solution.py:11
  38.8 7.4 %collective-permute-start.10 = (f32[8,4,16]{2,0,1:T(8,128)S(1)}, f32[8,4,16]{2,0,1:T(8,128)S(1)}, u32[]{:S(2)}, u32[]{:S(2)}) collective-permute-start(f32[8,4,16]{2,0,1:T(8,128)S(1)} %fusion.16), channel_id=1, source_target_pairs={{0,8},{4,12},{8,0},{12,4},{1,9},{5,13},{9,1},{13,5},{2,10},{6,14},... | collective-permute-start | bytes 6152 | tf_op jit(solution)/shard_map/ppermute | solution.py:11
  39.0 11.6 %collective-permute-start.7 = (bf16[8,4,16,128]{3,2,0,1:T(8,128)(2,1)S(1)}, bf16[8,4,16,128]{3,2,0,1:T(8,128)(2,1)S(1)}, u32[]{:S(2)}, u32[]{:S(2)}) collective-permute-start(bf16[8,4,16,128]{3,2,0,1:T(8,128)(2,1)S(1)} %fusion.81), channel_id=1, source_target_pairs={{0,8},{4,12},{8,0},{12,4},{1,9},{5,13},{9,1},{13,5},{2,10},{6,14},... | collective-permute-start | bytes 393224 | tf_op jit(solution)/shard_map/ppermute | solution.py:11
  42.1 6.7 %collective-permute-start.11 = (f32[8,4,16]{2,0,1:T(8,128)S(1)}, f32[8,4,16]{2,0,1:T(8,128)S(1)}, u32[]{:S(2)}, u32[]{:S(2)}) collective-permute-start(f32[8,4,16]{2,0,1:T(8,128)S(1)} %fusion.18), channel_id=1, source_target_pairs={{0,4},{4,8},{8,12},{12,0},{1,5},{5,9},{9,13},{13,1},{2,6},{6,10},{... | collective-permute-start | bytes 6152 | tf_op jit(solution)/shard_map/ppermute | solution.py:11
  43.3 7.3 %collective-permute-start.8 = (bf16[8,4,16,128]{3,2,0,1:T(8,128)(2,1)S(1)}, bf16[8,4,16,128]{3,2,0,1:T(8,128)(2,1)S(1)}, u32[]{:S(2)}, u32[]{:S(2)}) collective-permute-start(bf16[8,4,16,128]{3,2,0,1:T(8,128)(2,1)S(1)} %fusion.76), channel_id=1, source_target_pairs={{0,4},{4,8},{8,12},{12,0},{1,5},{5,9},{9,13},{13,1},{2,6},{6,10},{... | collective-permute-start | bytes 393224 | tf_op jit(solution)/shard_map/ppermute | solution.py:11
  51.9 53.5 %reduce-scatter.2.cloned.1.call-start = ((), (), s32[]{:S(2)}) async-start(), calls=%async_computation.2 | async-start | bytes 786432 | tf_op jit(solution)/shard_map/reduce_scatter | solution.py:79
Sparse Core Ops, SparseCore 0:
  52.0 21.2 all-gather.1
  91.1 14.2 reduce-scatter.1
where the time goes:
time: 114 us
  waiting for transfers between devices  47.8 us (42%)
  matrix products  28.6 us (25%)
  starting transfers between devices  15 us (13%)
  between operations  13.5 us (12%)
  other arithmetic  6.66 us (6%)
  local copies, waits for them, and re-layouts  2.15 us (2%)
    all_gather x1, waiting for transfers between devices, body(): gathered = lax.all_gather(attended, ('blk', 'rep'), axis=0, tiled=True)  21.4 us
    dot_general x1, matrix products, body(): jnp.dot(gathered, out_weight, preferred_element_type=jnp.float32)  17.6 us
    ppermute x12, starting transfers between devices, shifted(): lax.ppermute(x, axis, [(i, (i + by) % devices) for i in range(devices)])  15 us
    reduce_scatter x1, waiting for transfers between devices, body(): lax.psum_scatter(jnp.dot(gathered, out_weight, preferred_element_type=jnp...  14.4 us
    ppermute x12, waiting for transfers between devices, shifted(): lax.ppermute(x, axis, [(i, (i + by) % devices) for i in range(devices)])  12 us
    dot_general x4, matrix products, stop_partial(): jnp.einsum('rkgd,jkd->rkgj', queries, key_slot, preferred_element_type=jn...  6.02 us
    dot_general x4, matrix products, stop_partial(): jnp.einsum('rkgj,jkd->rkgd', weights.astype(jnp.bfloat16), value_slot, pr...  4.97 us
    reduce_sum x4, other arithmetic, stop_partial(): block_sum = jnp.sum(weights, axis=-1)  4.42 us
  transfers between devices with their start and end apart: 14, of which 7 were waited for; matrix products, arithmetic and copies ran while one was open for 12% of the time, Pallas kernels for 0%

commit v1 on v0

v1 whole, which is shorter than its diff:
```python
import functools
import jax
import jax.numpy as jnp
from jax import lax
from jax.experimental import pallas as pl
from jax.experimental.pallas import tpu as pltpu
from jax.sharding import PartitionSpec as P

NEG = -1e30
LOG2E = 1.4426950408889634
MESH = pl.DeviceIdType.MESH


def remote(src, dst, ssem, rsem, where):
    return pltpu.make_async_remote_copy(
        src_ref=src, dst_ref=dst, send_sem=ssem, recv_sem=rsem,
        device_id=where, device_id_type=MESH)


def kernel(
    dims, lengths, query, keys, values, weight, out,
    wv, kraw, vraw, kh, vt, fbuf, sbuf, wbuf, qbuf, qmat, pbuf, pstat, rbuf, rstat,
    abuf, acc, hsend, hrecv,
    wsem, ksem, q_ss, q_rs, p_ss, p_rs, t_ss, t_rs, a_ss, a_rs, c_ss, c_rs, h_ss, h_rs,
):
    B, R, H, S, stride, rows, K, G, HD, slab = dims
    heads = pl.ds
    group = G * rows
    lanes = S * group
    feat = G * HD
    cols = weight.shape[1]
    total = B * R * rows
    share = total // H
    nc = hsend.shape[1]
    cw = cols // nc
    scale2 = (HD ** -0.5) * LOG2E
    me_b = lax.axis_index("blk")
    me_r = lax.axis_index("rep")
    me_h = lax.axis_index("head")
    p = me_b // stride
    base = lax.rem(me_b, stride)

    def holder(q):
        return {"blk": q * stride + base}

    kcopy = pltpu.make_async_copy(keys, kraw, ksem.at[0])
    vcopy = pltpu.make_async_copy(values, vraw, ksem.at[1])
    kcopy.start()
    vcopy.start()
    wcopies = [
        pltpu.make_async_copy(weight.at[pl.ds(k * feat, feat)], wv.at[pl.ds(k * feat, feat)], wsem.at[k])
        for k in range(K)
    ]
    for c in wcopies:
        c.start()

    barrier = pltpu.get_barrier_semaphore()
    for d in range(1, S):
        pl.semaphore_signal(barrier, inc=1, device_id=holder(lax.rem(p + d, S)), device_id_type=MESH)
    for d in range(1, R):
        pl.semaphore_signal(barrier, inc=1, device_id={"rep": lax.rem(me_r + d, R)}, device_id_type=MESH)
    for d in range(1, H):
        pl.semaphore_signal(barrier, inc=1, device_id={"head": lax.rem(me_h + d, H)}, device_id_type=MESH)
    if stride > 1:
        for d in (1, B - 1):
            pl.semaphore_signal(barrier, inc=1, device_id={"blk": lax.rem(me_b + d, B)}, device_id_type=MESH)
    pl.semaphore_wait(barrier, (S - 1) + (R - 1) + (H - 1) + (2 if stride > 1 else 0))

    def q_move(k, o, side, src):
        to = p + 1 if side == 0 else p - 1
        return remote(src, qbuf.at[k, o], q_ss.at[k, o, side], q_rs.at[k, o], holder(to))

    def own_q(k):
        return query.at[:, pl.ds(k * feat, feat)]

    def q_start(k):
        @pl.when(p < S - 1)
        def _():
            q_move(k, p, 0, own_q(k)).start()

        @pl.when(p > 0)
        def _():
            q_move(k, p, 1, own_q(k)).start()

        qbuf[k, p] = query[:, k * feat:(k + 1) * feat]

    def q_hop(k, h):
        @pl.when(p >= h)
        def _():
            o = p - h
            q_move(k, o, 0, qbuf.at[k, o]).wait_recv()

            @pl.when(p < S - 1)
            def _():
                q_move(k, o, 0, qbuf.at[k, o]).start()

        @pl.when(p + h < S)
        def _():
            o = p + h
            q_move(k, o, 1, qbuf.at[k, o]).wait_recv()

            @pl.when(p > 0)
            def _():
                q_move(k, o, 1, qbuf.at[k, o]).start()

    def q_tick(t):
        if t < K:
            q_start(t)
        for h in range(S - 1, 0, -1):
            if 0 <= t - h < K:
                q_hop(t - h, h)

    def q_drain():
        for k in range(K):
            @pl.when(p < S - 1)
            def _():
                q_move(k, p, 0, own_q(k)).wait_send()
                for h in range(1, S):
                    @pl.when(p >= h)
                    def _():
                        q_move(k, p - h, 0, qbuf.at[k, p - h]).wait_send()

            @pl.when(p > 0)
            def _():
                q_move(k, p, 1, own_q(k)).wait_send()
                for h in range(1, S):
                    @pl.when(p + h < S)
                    def _():
                        q_move(k, p + h, 1, qbuf.at[k, p + h]).wait_send()

    sub = lax.rem(lax.broadcasted_iota(jnp.int32, (1, group), 1), rows)
    pieces = []
    for o in range(S):
        first = ((o * stride + base) * R + me_r) * rows
        piece = jnp.zeros((1, group), jnp.int32)
        for r in range(rows):
            piece = jnp.where(sub == r, lengths[first + r], piece)
        pieces.append(piece)
    live_to = jnp.concatenate(pieces, axis=1) - p * slab

    step = 256

    def split(c, carry):
        src = pl.ds(pl.multiple_of(c * step * K, step * K), step * K)
        dst = pl.ds(pl.multiple_of(c * step, step), step)
        fbuf[0] = kraw[src, :].astype(jnp.float32)
        fbuf[1] = vraw[src, :].astype(jnp.float32)
        for k in range(K):
            kh[k, dst, :] = fbuf[0, pl.ds(k, step, stride=K), :].astype(jnp.bfloat16)
            vt[k, :, dst] = fbuf[1, pl.ds(k, step, stride=K), :].T.astype(jnp.bfloat16)
        return carry

    def attend(k):
        for o in range(S):
            x = qbuf[k, o].astype(jnp.float32)
            x = jnp.concatenate([x[:, g * HD:(g + 1) * HD] for g in range(G)], axis=0)
            qmat[o * group:(o + 1) * group, :] = x.astype(jnp.bfloat16)
        qk = qmat[...]
        iota = lax.broadcasted_iota(jnp.int32, (step, lanes), 0)

        def first(c, m):
            at = pl.ds(pl.multiple_of(c * step, step), step)
            s = lax.dot_general(kh[k, at, :], qk, (((1,), (1,)), ((), ())), preferred_element_type=jnp.float32)
            s = jnp.where(iota < live_to - c * step, s, NEG)
            sbuf[at, :] = s
            return jnp.maximum(m, jnp.max(s.reshape(step // 8, 8, lanes), axis=0))

        m = lax.fori_loop(0, slab // step, first, jnp.full((8, lanes), NEG, jnp.float32))
        m = jnp.max(m, axis=0, keepdims=True)

        def second(c, l):
            at = pl.ds(pl.multiple_of(c * step, step), step)
            e = jnp.exp2((sbuf[at, :] - m) * scale2)
            wbuf[at, :] = e.astype(jnp.bfloat16)
            return l + jnp.sum(e.reshape(step // 8, 8, lanes), axis=0)

        l = lax.fori_loop(0, slab // step, second, jnp.zeros((8, lanes), jnp.float32))
        l = jnp.sum(l, axis=0, keepdims=True)
        part = jnp.dot(vt[k], wbuf[...], preferred_element_type=jnp.float32).astype(jnp.bfloat16)
        four = jnp.zeros((4, group), jnp.float32)
        for o in range(S):
            at = slice(o * group, (o + 1) * group)
            pbuf[k, o] = part[:, at]
            pstat[k, o, 0:1] = m[:, at]
            pstat[k, o, 1:2] = l[:, at]

    def p_move(k, to, frm):
        return (
            remote(pbuf.at[k, to], rbuf.at[k, frm], p_ss.at[k, to], p_rs.at[k, frm], holder(to)),
            remote(pstat.at[k, to], rstat.at[k, frm], t_ss.at[k, to], t_rs.at[k, frm], holder(to)),
        )

    def p_send(k):
        for d in range(1, S):
            for c in p_move(k, lax.rem(p + d, S), p):
                c.start()
        rbuf[k, p] = pbuf[k, p]
        rstat[k, p] = pstat[k, p]

    def a_line(k, o, side):
        to = me_b + 1 if side == 0 else me_b - 1
        slot = abuf.at[k, o * R + me_r]
        return remote(slot, slot, a_ss.at[k, o, side], a_rs.at[k, o], {"blk": to})

    def a_core(k, o, d):
        slot = abuf.at[k, o * R + me_r]
        return remote(slot, slot, c_ss.at[k, o, d - 1], c_rs.at[k, o, d - 1], {"rep": lax.rem(me_r + d, R)})

    def a_core_in(k, o, d):
        slot = abuf.at[k, o * R + lax.rem(me_r + R - d, R)]
        return remote(slot, slot, c_ss.at[k, o, d - 1], c_rs.at[k, o, d - 1], {"rep": lax.rem(me_r + d, R)})

    def combine(k):
        for d in range(1, S):
            for c in p_move(k, lax.rem(p + d, S), lax.rem(p + S - d, S)):
                c.wait_recv()
        best = [rstat[k, s, 0:1] for s in range(S)]
        top = functools.reduce(jnp.maximum, best)
        den = jnp.zeros((1, group), jnp.float32)
        num = jnp.zeros((HD, group), jnp.float32)
        for s in range(S):
            f = jnp.exp2((best[s] - top) * scale2)
            den = den + f * rstat[k, s, 1:2]
            num = num + f * rbuf[k, s].astype(jnp.float32)
        att = (num / den).T
        att = jnp.concatenate([att[g * rows:(g + 1) * rows, :] for g in range(G)], axis=1)
        abuf[k, me_b * R + me_r] = att.astype(jnp.bfloat16)

        @pl.when(me_b < B - 1)
        def _():
            a_line(k, me_b, 0).start()

        @pl.when(me_b > 0)
        def _():
            a_line(k, me_b, 1).start()

        for d in range(1, R):
            a_core(k, me_b, d).start()

    def a_hop(k, h):
        @pl.when(me_b >= h)
        def _():
            o = me_b - h
            a_line(k, o, 0).wait_recv()

            @pl.when(me_b < B - 1)
            def _():
                a_line(k, o, 0).start()

            for d in range(1, R):
                a_core(k, o, d).start()

        @pl.when(me_b + h < B)
        def _():
            o = me_b + h
            a_line(k, o, 1).wait_recv()

            @pl.when(me_b > 0)
            def _():
                a_line(k, o, 1).start()

            for d in range(1, R):
                a_core(k, o, d).start()

    def a_drain():
        for k in range(K):
            for o in range(B):
                for d in range(1, R):
                    a_core(k, o, d).wait_send()

            @pl.when(me_b < B - 1)
            def _():
                for o in range(B):
                    @pl.when(me_b >= o)
                    def _():
                        a_line(k, o, 0).wait_send()

            @pl.when(me_b > 0)
            def _():
                for o in range(B):
                    @pl.when(me_b <= o)
                    def _():
                        a_line(k, o, 1).wait_send()

    def h_move(n, d):
        return remote(hsend.at[d - 1, n], hrecv.at[d - 1, n], h_ss.at[d - 1, n], h_rs.at[d - 1, n],
                      {"head": lax.rem(me_h + d, H)})

    def project(k):
        wcopies[k].wait()
        for o in range(B):
            for d in range(1, R):
                a_core_in(k, o, d).wait_recv()
        rowsk = jnp.concatenate([abuf[k, i].astype(jnp.float32) for i in range(B * R)], axis=0).astype(jnp.bfloat16)
        for n in range(nc):
            w = wv[k * feat:(k + 1) * feat, n * cw:(n + 1) * cw]
            y = jnp.dot(rowsk, w, preferred_element_type=jnp.float32)
            if k > 0:
                y = y + acc[n]
            acc[n] = y
            if k == K - 1:
                for d in range(1, H):
                    to = lax.rem(me_h + d, H)
                    hsend[d - 1, n] = acc[n, pl.ds(pl.multiple_of(to * share, share), share), :].astype(jnp.bfloat16)
                    h_move(n, d).start()

    q_tick(0)
    kcopy.wait()
    vcopy.wait()
    lax.fori_loop(0, slab // step, split, 0)
    for t in range(1, S):
        q_tick(t)
    done_hops = []
    todo = []

    for k in range(K):
        attend(k)
        p_send(k)
        if k + 1 < K:
            q_tick(S + k)
        if k >= 2:
            a_hop(k - 2, 1)
        if k >= 1:
            combine(k - 1)
        if k >= 3:
            for h in range(2, B):
                a_hop(k - 3, h)
            project(k - 3)
    combine(K - 1)
    left = list(range(max(0, K - 3), K))
    for k in left:
        if k > K - 3 or K < 3:
            a_hop(k, 1)
    for k in left:
        for h in range(2, B):
            a_hop(k, h)
        project(k)
    own = pl.ds(pl.multiple_of(me_h * share, share), share)
    for n in range(nc):
        y = acc[n, own, :]
        for d in range(1, H):
            h_move(n, d).wait_recv()
            y = y + hrecv[d - 1, n].astype(jnp.float32)
        out[:, n * cw:(n + 1) * cw] = y.astype(jnp.bfloat16)
    q_drain()
    for k in range(K):
        for d in range(1, S):
            for c in p_move(k, lax.rem(p + d, S), p):
                c.wait_send()
    a_drain()
    for n in range(nc):
        for d in range(1, H):
            h_move(n, d).wait_send()


def body(query, keys, values, lengths, out_weight):
    rows = query.shape[0]
    slab, K, HD = keys.shape[2:]
    B = lax.axis_size("blk")
    R = lax.axis_size("rep")
    H = lax.axis_size("head")
    S = min(8, B)
    stride = B // S
    G = query.shape[1] // (K * HD)
    feat = G * HD
    group = G * rows
    lanes = S * group
    depth, cols = out_weight.shape
    total = B * R * rows
    share = total // H
    nc = max(1, cols // 512)
    cw = cols // nc
    dims = (B, R, H, S, stride, rows, K, G, HD, slab)
    bf, f32 = jnp.bfloat16, jnp.float32
    vm, dma = pltpu.VMEM, pltpu.SemaphoreType.DMA
    any_spec = pl.BlockSpec(memory_space=pltpu.HBM)
    return pl.pallas_call(
        functools.partial(kernel, dims),
        out_shape=jax.ShapeDtypeStruct((share, cols), bf),
        in_specs=[
            pl.BlockSpec(memory_space=pltpu.SMEM),
            pl.BlockSpec(memory_space=pltpu.VMEM),
            any_spec, any_spec, any_spec,
        ],
        out_specs=pl.BlockSpec(memory_space=pltpu.VMEM),
        scratch_shapes=[
            vm((depth, cols), bf),
            vm((slab * K, HD), bf),
            vm((slab * K, HD), bf),
            vm((K, slab, HD), bf),
            vm((K, HD, slab), bf),
            vm((2, 256 * K, HD), f32),
            vm((slab, lanes), f32),
            vm((slab, lanes), bf),
            vm((K, S, rows, feat), bf),
            vm((lanes, HD), bf),
            vm((K, S, HD, group), bf),
            vm((K, S, 8, group), f32),
            vm((K, S, HD, group), bf),
            vm((K, S, 8, group), f32),
            vm((K, B * R, rows, feat), bf),
            vm((nc, total, cw), f32),
            vm((max(1, H - 1), nc, share, cw), bf),
            vm((max(1, H - 1), nc, share, cw), bf),
            dma((K,)),
            dma((2,)),
            dma((K, S, 2)), dma((K, S)),
            dma((K, S)), dma((K, S)),
            dma((K, S)), dma((K, S)),
            dma((K, B, 2)), dma((K, B)),
            dma((K, B, max(1, R - 1))), dma((K, B, max(1, R - 1))),
            dma((max(1, H - 1), nc)), dma((max(1, H - 1), nc)),
        ],
        compiler_params=pltpu.CompilerParams(
            collective_id=0, has_side_effects=True, vmem_limit_bytes=61 * 1024 * 1024),
        name="attend_project",
    )(lengths, query, keys.reshape(slab * K, HD), values.reshape(slab * K, HD), out_weight)


def solution(mesh):
    return jax.shard_map(
        body,
        mesh=mesh,
        in_specs=(
            P(("groups", "blk", "rep"), "head"),
            P(("groups", "blk"), "rep", None, "head", None),
            P(("groups", "blk"), "rep", None, "head", None),
            P("groups"),
            P("head", ("blk", "rep")),
        ),
        out_specs=P(("groups", "head"), ("blk", "rep")),
        check_vma=False,
    )
```

time: 114 us -> 67.4 us (0.59)
  Pallas kernels: 0 us -> 65.7 us
  waiting for transfers between devices: 47.8 us -> 0 us
  matrix products: 28.6 us -> 0 us
  starting transfers between devices: 15 us -> 0 us
  between operations: 13.5 us -> 0.01 us
  other arithmetic: 6.66 us -> 0 us
    pallas_call x0 -> x1, Pallas kernels: none -> 65.7 us  [body(): pl.pallas_call(functools.partial(kernel, dims), out_shape=jax.ShapeDtypeS...]
    dot_general x9 -> x0, matrix products: 28.6 us -> none  [the longest x1 17.6 us: body(): jnp.dot(gathered, out_weight, preferred_element_type=jnp.float32)]
    all_gather x1 -> x0, waiting for transfers between devices: 21.4 us -> none  [body(): gathered = lax.all_gather(attended, ('blk', 'rep'), axis=0, tiled=True)]
    ppermute x12 -> x0, starting transfers between devices: 15 us -> none  [shifted(): lax.ppermute(x, axis, [(i, (i + by) % devices) for i in range(devices)])]
    reduce_scatter x1 -> x0, waiting for transfers between devices: 14.4 us -> none  [body(): lax.psum_scatter(jnp.dot(gathered, out_weight, preferred_element_type=jnp...]
    ppermute x12 -> x0, waiting for transfers between devices: 12 us -> none  [shifted(): lax.ppermute(x, axis, [(i, (i + by) % devices) for i in range(devices)])]
    reduce_sum x6 -> x0, other arithmetic: 4.78 us -> none  [the longest x4 4.42 us: stop_partial(): block_sum = jnp.sum(weights, axis=-1)]
    convert_element_type x2 -> x0, other arithmetic: 1.76 us -> none  [the longest x1 1.62 us: body(): return projected.astype(jnp.bfloat16)]
  transfers between devices with their start and end apart: 14 -> 0, of which waited for: 7 -> 0; matrix products, arithmetic and copies ran while one was open for 12% -> 0% of each run, Pallas kernels for 0% -> 0%
where the time goes in v1:
time: 67.4 us; the launch traced here: 67.2 us
  Pallas kernels  65.7 us (97%)
  local copies, waits for them, and re-layouts  1.57 us (2%)
    pallas_call x1, Pallas kernels, body(): pl.pallas_call(functools.partial(kernel, dims), out_shape=jax.ShapeDtypeS...  65.7 us
    unnamed x1, local copies, waits for them, and re-layouts  1.57 us

profile of v1, /device:TPU:0, one launch (start us, length us, event | category | flops | bytes accessed | tf_op | source)
XLA Modules:
  0.0 67.2 jit_solution(5959250423709359577)
XLA Ops:
  0.0 65.7 %attend_project.1 = bf16[32,2048]{1,0:T(8,128)(2,1)} custom-call(s32[64]{0:T(128)} %lengths.1, bf16[8,8192]{1,0:T(8,128)(2,1)} %query.1, bf16[8192,128]{1,0:T(8,128)(2,1)} %bitcast.2, bf16[8192,128]{1,0:T(8,128)(2,1)} %bitcast.3, bf16[8192,2048]{1,0:T(8,128)(2,1)} %weight.1), custom_call_target="tpu_custom_call" | custom-call | tf_op jit(solution)/shard_map/attend_project/pallas_call | solution.py:377
  65.7 1.6 %copy.7 = bf16[32,2048]{1,0:T(8,128)(2,1)} copy(bf16[32,2048]{1,0:T(8,128)(2,1)} %attend_project.1) | data formatting | bytes 262144

commit v2 on v1

--- a/solution.py
+++ b/solution.py
@@ -20,8 +20,9 @@
 def kernel(
     dims, lengths, query, keys, values, weight, out,
     wv, kraw, vraw, kh, vt, fbuf, sbuf, wbuf, qbuf, qmat, pbuf, pstat, rbuf, rstat,
-    abuf, acc, hsend, hrecv,
+    abuf, acc, hsend, hrecv, lin, lstat, lout, lostat,
     wsem, ksem, q_ss, q_rs, p_ss, p_rs, t_ss, t_rs, a_ss, a_rs, c_ss, c_rs, h_ss, h_rs,
+    l_ss, l_rs, s_ss, s_rs,
 ):
     B, R, H, S, stride, rows, K, G, HD, slab = dims
     heads = pl.ds
@@ -51,8 +52,6 @@
         pltpu.make_async_copy(weight.at[pl.ds(k * feat, feat)], wv.at[pl.ds(k * feat, feat)], wsem.at[k])
         for k in range(K)
     ]
-    for c in wcopies:
-        c.start()
 
     barrier = pltpu.get_barrier_semaphore()
     for d in range(1, S):
@@ -103,12 +102,12 @@
             def _():
                 q_move(k, o, 1, qbuf.at[k, o]).start()
 
-    def q_tick(t):
-        if t < K:
-            q_start(t)
-        for h in range(S - 1, 0, -1):
-            if 0 <= t - h < K:
-                q_hop(t - h, h)
+    hops = sorted((k + 2 * h, h, k) for k in range(K) for h in range(1, S))
+
+    def q_ready(k):
+        while hops and hops[0][0] <= k + 2 * (S - 1):
+            _, h, j = hops.pop(0)
+            q_hop(j, h)
 
     def q_drain():
         for k in range(K):
@@ -165,7 +164,7 @@
             sbuf[at, :] = s
             return jnp.maximum(m, jnp.max(s.reshape(step // 8, 8, lanes), axis=0))
 
-        m = lax.fori_loop(0, slab // step, first, jnp.full((8, lanes), NEG, jnp.float32))
+        m = lax.fori_loop(0, slab // step, first, jnp.full((8, lanes), NEG, jnp.float32), unroll=2)
         m = jnp.max(m, axis=0, keepdims=True)
 
         def second(c, l):
@@ -174,10 +173,9 @@
             wbuf[at, :] = e.astype(jnp.bfloat16)
             return l + jnp.sum(e.reshape(step // 8, 8, lanes), axis=0)
 
-        l = lax.fori_loop(0, slab // step, second, jnp.zeros((8, lanes), jnp.float32))
+        l = lax.fori_loop(0, slab // step, second, jnp.zeros((8, lanes), jnp.float32), unroll=2)
         l = jnp.sum(l, axis=0, keepdims=True)
         part = jnp.dot(vt[k], wbuf[...], preferred_element_type=jnp.float32).astype(jnp.bfloat16)
-        four = jnp.zeros((4, group), jnp.float32)
         for o in range(S):
             at = slice(o * group, (o + 1) * group)
             pbuf[k, o] = part[:, at]
@@ -304,37 +302,129 @@
                     hsend[d - 1, n] = acc[n, pl.ds(pl.multiple_of(to * share, share), share), :].astype(jnp.bfloat16)
                     h_move(n, d).start()
 
-    q_tick(0)
+    near = jnp.where(p < S // 2, 0, 1)
+
+    def line_move(w, k, o, acc_src, stat_src):
+        to = holder(p + 1 - 2 * w)
+        return (
+            remote(acc_src, lin.at[w, k, o], l_ss.at[w, k, o], l_rs.at[w, k, o], to),
+            remote(stat_src, lstat.at[w, k, o], s_ss.at[w, k, o], s_rs.at[w, k, o], to),
+        )
+
+    def line_source(k, o):
+        @pl.when(p == 0)
+        def _():
+            for c in line_move(0, k, o, pbuf.at[k, o], pstat.at[k, o]):
+                c.start()
+
+        @pl.when(p == S - 1)
+        def _():
+            for c in line_move(1, k, o, pbuf.at[k, o], pstat.at[k, o]):
+                c.start()
+
+    def line_step(w, k, o):
+        @pl.when((p > 0) & (p < S - 1))
+        def _():
+            for c in line_move(w, k, o, lout.at[w, k, o], lostat.at[w, k, o]):
+                c.wait_recv()
+            m_in, m_own = lstat[w, k, o, 0:1], pstat[k, o, 0:1]
+            top = jnp.maximum(m_in, m_own)
+            f_in, f_own = jnp.exp2((m_in - top) * scale2), jnp.exp2((m_own - top) * scale2)
+            lout[w, k, o] = (
+                f_in * lin[w, k, o].astype(jnp.float32) + f_own * pbuf[k, o].astype(jnp.float32)
+            ).astype(jnp.bfloat16)
+            lostat[w, k, o, 0:1] = top
+            lostat[w, k, o, 1:2] = f_in * lstat[w, k, o, 1:2] + f_own * pstat[k, o, 1:2]
+            for c in line_move(w, k, o, lout.at[w, k, o], lostat.at[w, k, o]):
+                c.start()
+
+    def line_final(k, o):
+        @pl.when(p == 0)
+        def _():
+            for c in line_move(1, k, o, lout.at[1, k, o], lostat.at[1, k, o]):
+                c.wait_recv()
+
+        @pl.when(p == S - 1)
+        def _():
+            for c in line_move(0, k, o, lout.at[0, k, o], lostat.at[0, k, o]):
+                c.wait_recv()
+
+        stats = [pstat[k, o], lstat[0, k, o], lstat[1, k, o]]
+        accs = [pbuf[k, o], lin[0, k, o], lin[1, k, o]]
+        top = functools.reduce(jnp.maximum, [x[0:1] for x in stats])
+        den = jnp.zeros((1, group), jnp.float32)
+        num = jnp.zeros((HD, group), jnp.float32)
+        for x, y in zip(stats, accs):
+            f = jnp.exp2((x[0:1] - top) * scale2)
+            den = den + f * x[1:2]
+            num = num + f * y.astype(jnp.float32)
+        att = (num / den).T
+        att = jnp.concatenate([att[g * rows:(g + 1) * rows, :] for g in range(G)], axis=1)
+        abuf[k, o * R + me_r] = att.astype(jnp.bfloat16)
+        for d in range(1, R):
+            a_core(k, o, d).start()
+
+    def line_drain():
+        for k in range(K):
+            for o in range(S):
+                for w in range(2):
+                    @pl.when(p != (S - 1) * (1 - w))
+                    def _():
+                        for c in line_move(w, k, o, pbuf.at[k, o], pstat.at[k, o]):
+                            c.wait_send()
+                for d in range(1, R):
+                    a_core(k, o, d).wait_send()
+
+    early = max(1, K - 1)
+    for k in range(early):
+        q_start(k)
+    if stride == 1:
+        for w in range(2):
+            @pl.when(p == (S - 1) * w)
+            def _():
+                for k in range(K):
+                    for o in range(S):
+                        lin[w, k, o] = jnp.zeros((HD, group), jnp.bfloat16)
+                        lstat[w, k, o, 0:1] = jnp.full((1, group), NEG, jnp.float32)
+                        lstat[w, k, o, 1:2] = jnp.zeros((1, group), jnp.float32)
     kcopy.wait()
     vcopy.wait()
     lax.fori_loop(0, slab // step, split, 0)
-    for t in range(1, S):
-        q_tick(t)
-    done_hops = []
-    todo = []
-
-    for k in range(K):
-        attend(k)
-        p_send(k)
-        if k + 1 < K:
-            q_tick(S + k)
-        if k >= 2:
-            a_hop(k - 2, 1)
-        if k >= 1:
-            combine(k - 1)
-        if k >= 3:
-            for h in range(2, B):
-                a_hop(k - 3, h)
-            project(k - 3)
-    combine(K - 1)
-    left = list(range(max(0, K - 3), K))
-    for k in left:
-        if k > K - 3 or K < 3:
-            a_hop(k, 1)
-    for k in left:
-        for h in range(2, B):
-            a_hop(k, h)
-        project(k)
+    if S > 1 and K > early:
+        _, h, j = hops.pop(0)
+        q_hop(j, h)
+    for k in range(early, K):
+        q_start(k)
+    if stride == 1:
+        for t in range(K + 4):
+            if t < K:
+                q_ready(t)
+                wcopies[t].start()
+                attend(t)
+                for o in range(S):
+                    line_source(t, o)
+            for o in range(S):
+                if 0 <= t - 1 < K:
+                    line_step(near, t - 1, o)
+                if 0 <= t - 2 < K:
+                    line_step(1 - near, t - 2, o)
+            if 0 <= t - 3 < K:
+                for o in range(S):
+                    line_final(t - 3, o)
+            if 0 <= t - 4 < K:
+                project(t - 4)
+    else:
+        for k in range(K):
+            q_ready(k)
+            wcopies[k].start()
+            attend(k)
+            p_send(k)
+        for k in range(K):
+            combine(k)
+        for k in range(K):
+            for h in range(1, B):
+                a_hop(k, h)
+            project(k)
     own = pl.ds(pl.multiple_of(me_h * share, share), share)
     for n in range(nc):
         y = acc[n, own, :]
@@ -343,11 +433,14 @@
             y = y + hrecv[d - 1, n].astype(jnp.float32)
         out[:, n * cw:(n + 1) * cw] = y.astype(jnp.bfloat16)
     q_drain()
-    for k in range(K):
-        for d in range(1, S):
-            for c in p_move(k, lax.rem(p + d, S), p):
-                c.wait_send()
-    a_drain()
+    if stride == 1:
+        line_drain()
+    else:
+        for k in range(K):
+            for d in range(1, S):
+                for c in p_move(k, lax.rem(p + d, S), p):
+                    c.wait_send()
+        a_drain()
     for n in range(nc):
         for d in range(1, H):
             h_move(n, d).wait_send()
@@ -370,6 +463,7 @@
     share = total // H
     nc = max(1, cols // 512)
     cw = cols // nc
+    line = (2, K, S) if stride == 1 else (1, 1, 1)
     dims = (B, R, H, S, stride, rows, K, G, HD, slab)
     bf, f32 = jnp.bfloat16, jnp.float32
     vm, dma = pltpu.VMEM, pltpu.SemaphoreType.DMA
@@ -395,13 +489,17 @@
             vm((K, S, rows, feat), bf),
             vm((lanes, HD), bf),
             vm((K, S, HD, group), bf),
-            vm((K, S, 8, group), f32),
+            vm((K, S, 2, group), f32),
             vm((K, S, HD, group), bf),
-            vm((K, S, 8, group), f32),
+            vm((K, S, 2, group), f32),
             vm((K, B * R, rows, feat), bf),
             vm((nc, total, cw), f32),
             vm((max(1, H - 1), nc, share, cw), bf),
             vm((max(1, H - 1), nc, share, cw), bf),
+            vm(line + (HD, group), bf),
+            vm(line + (2, group), f32),
+            vm(line + (HD, group), bf),
+            vm(line + (2, group), f32),
             dma((K,)),
             dma((2,)),
             dma((K, S, 2)), dma((K, S)),
@@ -410,6 +508,7 @@
             dma((K, B, 2)), dma((K, B)),
             dma((K, B, max(1, R - 1))), dma((K, B, max(1, R - 1))),
             dma((max(1, H - 1), nc)), dma((max(1, H - 1), nc)),
+            dma(line), dma(line), dma(line), dma(line),
         ],
         compiler_params=pltpu.CompilerParams(
             collective_id=0, has_side_effects=True, vmem_limit_bytes=61 * 1024 * 1024),

time: 67.4 us -> 51.4 us (0.76)
  Pallas kernels: 65.7 us -> 49.7 us
    pallas_call x1, Pallas kernels: 65.7 us -> 49.7 us  [body(): pl.pallas_call(functools.partial(kernel, dims), out_shape=jax.ShapeDtypeS...]
where the time goes in v2:
time: 51.4 us; the launch traced here: 51.3 us
  Pallas kernels  49.7 us (97%)
  local copies, waits for them, and re-layouts  1.57 us (3%)
    pallas_call x1, Pallas kernels, body(): pl.pallas_call(functools.partial(kernel, dims), out_shape=jax.ShapeDtypeS...  49.7 us
    unnamed x1, local copies, waits for them, and re-layouts  1.57 us

profile of v2, /device:TPU:0, one launch (start us, length us, event | category | flops | bytes accessed | tf_op | source)
XLA Modules:
  0.0 51.3 jit_solution(3051290000152491160)
XLA Ops:
  0.0 49.7 %attend_project.1 = bf16[32,2048]{1,0:T(8,128)(2,1)} custom-call(s32[64]{0:T(128)} %lengths.1, bf16[8,8192]{1,0:T(8,128)(2,1)} %query.1, bf16[8192,128]{1,0:T(8,128)(2,1)} %bitcast.2, bf16[8192,128]{1,0:T(8,128)(2,1)} %bitcast.3, bf16[8192,2048]{1,0:T(8,128)(2,1)} %weight.1), custom_call_target="tpu_custom_call" | custom-call | tf_op jit(solution)/shard_map/attend_project/pallas_call | solution.py:471
  49.7 1.6 %copy.7 = bf16[32,2048]{1,0:T(8,128)(2,1)} copy(bf16[32,2048]{1,0:T(8,128)(2,1)} %attend_project.1) | data formatting | bytes 262144

commit v3 on v2

--- a/solution.py
+++ b/solution.py
@@ -164,7 +164,7 @@
             sbuf[at, :] = s
             return jnp.maximum(m, jnp.max(s.reshape(step // 8, 8, lanes), axis=0))
 
-        m = lax.fori_loop(0, slab // step, first, jnp.full((8, lanes), NEG, jnp.float32), unroll=2)
+        m = lax.fori_loop(0, slab // step, first, jnp.full((8, lanes), NEG, jnp.float32), unroll=4)
         m = jnp.max(m, axis=0, keepdims=True)
 
         def second(c, l):
@@ -173,7 +173,7 @@
             wbuf[at, :] = e.astype(jnp.bfloat16)
             return l + jnp.sum(e.reshape(step // 8, 8, lanes), axis=0)
 
-        l = lax.fori_loop(0, slab // step, second, jnp.zeros((8, lanes), jnp.float32), unroll=2)
+        l = lax.fori_loop(0, slab // step, second, jnp.zeros((8, lanes), jnp.float32), unroll=4)
         l = jnp.sum(l, axis=0, keepdims=True)
         part = jnp.dot(vt[k], wbuf[...], preferred_element_type=jnp.float32).astype(jnp.bfloat16)
         for o in range(S):
@@ -399,10 +399,11 @@
         for t in range(K + 4):
             if t < K:
                 q_ready(t)
-                wcopies[t].start()
                 attend(t)
                 for o in range(S):
                     line_source(t, o)
+            if 0 <= t - 1 < K:
+                wcopies[t - 1].start()
             for o in range(S):
                 if 0 <= t - 1 < K:
                     line_step(near, t - 1, o)

time: 51.4 us -> 50.4 us (0.981)
  Pallas kernels: 49.7 us -> 48.7 us
    pallas_call x1, Pallas kernels: 49.7 us -> 48.7 us  [body(): pl.pallas_call(functools.partial(kernel, dims), out_shape=jax.ShapeDtypeS...]
where the time goes in v3:
time: 50.4 us; the launch traced here: 50.2 us
  Pallas kernels  48.7 us (97%)
  local copies, waits for them, and re-layouts  1.57 us (3%)
    pallas_call x1, Pallas kernels, body(): pl.pallas_call(functools.partial(kernel, dims), out_shape=jax.ShapeDtypeS...  48.7 us
    unnamed x1, local copies, waits for them, and re-layouts  1.57 us

profile of v3, /device:TPU:0, one launch (start us, length us, event | category | flops | bytes accessed | tf_op | source)
XLA Modules:
  0.0 50.2 jit_solution(5871605845209391486)
XLA Ops:
  0.0 48.7 %attend_project.1 = bf16[32,2048]{1,0:T(8,128)(2,1)} custom-call(s32[64]{0:T(128)} %lengths.1, bf16[8,8192]{1,0:T(8,128)(2,1)} %query.1, bf16[8192,128]{1,0:T(8,128)(2,1)} %bitcast.2, bf16[8192,128]{1,0:T(8,128)(2,1)} %bitcast.3, bf16[8192,2048]{1,0:T(8,128)(2,1)} %weight.1), custom_call_target="tpu_custom_call" | custom-call | tf_op jit(solution)/shard_map/attend_project/pallas_call | solution.py:472
  48.7 1.6 %copy.7 = bf16[32,2048]{1,0:T(8,128)(2,1)} copy(bf16[32,2048]{1,0:T(8,128)(2,1)} %attend_project.1) | data formatting | bytes 262144
